TPU v7x, 256 devices: a whole 4x4x8 slice. The times are simulated.
256 devices in a mesh: row: 16 (over x, y), col: 16 (over z, core).
Axes of the slice: x: 4, y: 4, z: 8, core: 2. Of those that a mesh axis runs over, the one named last changes fastest.
Arguments:
- density: bfloat16 [24576, 24576], P('col', 'row')
- margin: bfloat16 [24576, 24576], P('row', 'col')
- density_mask: int32 [192, 192], P('col', 'row'), may hold values from 0 to 1, as said below
- margin_mask: int32 [192, 192], P('row', 'col'), may hold values from 0 to 1, as said below
- keep_mask: int32 [3, 192], replicated, may hold values 0 or 1
Outputs:
- purified: bfloat16 [384, 24576], P('col', 'row')
Inputs may be any that keep to these rules, and one draw needn't show every extreme that they name: `density_mask`: block (i, j) is 1 where |i - j| <= 1 and 0 where |i - j| >= 96. `margin_mask`: block (i, j) is 1 where |i - j| <= 1 and 0 where |i - j| >= 96.
All inputs are finite; a program needn't handle non-finite values.
Results may differ from a plain program's by a relative error of at most 0.008.
Values may be sent and summed in bfloat16 or wider, within the bound.
No kernel may reach another device: no remote copies, remote signals or barrier semaphores. Data moves between devices by JAX's collectives and lax.ppermute only.
A program may use at most 64 MiB of HBM per device.

v0:
```python
import jax
import jax.numpy as jnp
from jax import lax
from jax.experimental import pallas as pl
from jax.experimental.pallas import tpu as pltpu
from jax.sharding import Mesh, PartitionSpec as P


BLK = 128
SLAB_BLK = 3
NX, NY, NZ, NC = 4, 4, 8, 2
ROW = ("x", "y")
BF = jnp.bfloat16
F32 = jnp.float32
SMALL = 8 * 1024 * 1024
ORDER = (1, 2, 3, 6, 5, 7, 4)


def slab_kernel(piece, pattern_ref, tile_ref, first_ref, second_ref, held, sems):
    @pl.when(lax.axis_index("z") == 0)
    def _():
        rows, cols = held.shape
        parts = rows // BLK
        copies = []
        for p in range(parts):
            span = pl.ds(p * BLK, BLK)
            copies.append(pltpu.make_async_copy(tile_ref.at[span], held.at[span], sems.at[p]))
            copies[-1].start()
        for p in range(parts):
            copies[p].wait()
            stored = [pattern_ref[p, j] > 0 for j in range(cols // BLK)]
            for row in range(p * BLK, (p + 1) * BLK, 8):
                whose, at = divmod(row, piece)
                z, core = divmod(whose, NC)
                out_ref = (first_ref, second_ref)[core]
                for j in range(cols // BLK):
                    lanes = slice(j * BLK, (j + 1) * BLK)
                    block = held[row : row + 8, lanes]
                    out_ref[z, at : at + 8, lanes] = jnp.where(stored[j], block, jnp.zeros_like(block))


def slab_halves(tile, pattern, slab, piece):
    cols = tile.shape[1]
    return pl.pallas_call(
        lambda *refs: slab_kernel(piece, *refs),
        in_specs=[
            pl.BlockSpec(memory_space=pltpu.SMEM),
            pl.BlockSpec(memory_space=pltpu.HBM),
        ],
        out_specs=[pl.BlockSpec(memory_space=pltpu.VMEM)] * NC,
        out_shape=[pltpu.VMEM((NZ, piece, cols), BF)] * NC,
        scratch_shapes=[pltpu.VMEM((slab, cols), BF), pltpu.SemaphoreType.DMA((SLAB_BLK,))],
        compiler_params=pltpu.CompilerParams(vmem_limit_bytes=SMALL),
        name="slab",
    )(pattern, pltpu.with_memory_space_constraint(tile, pltpu.HBM))


def load_kernel(with_diag, pattern_ref, where_ref, left_ref, right_ref, out_ref, held, sems):
    depth, width = held.shape
    parts = sems.shape[0]
    wide = width // parts
    copies = [
        pltpu.make_async_copy(
            right_ref.at[:, pl.ds(j * wide, wide)], held.at[:, pl.ds(j * wide, wide)], sems.at[j]
        )
        for j in range(parts)
    ]
    copies[0].start()
    copies[1].start()
    for p in range(parts):
        copies[p].wait()
        if p + 2 < parts:
            copies[p + 2].start()
        for j in range(p * wide // BLK, (p + 1) * wide // BLK):
            for i in range(depth // BLK):
                here = (slice(i * BLK, (i + 1) * BLK), slice(j * BLK, (j + 1) * BLK))

                @pl.when(pattern_ref[i, j] <= 0)
                def _():
                    held[here] = jnp.zeros((BLK, BLK), BF)

                if with_diag and i == j:

                    @pl.when(where_ref[0] == where_ref[1])
                    def _():
                        eye = (
                            lax.broadcasted_iota(jnp.int32, (BLK, BLK), 0)
                            == lax.broadcasted_iota(jnp.int32, (BLK, BLK), 1)
                        ).astype(F32)
                        held[here] = (held[here].astype(F32) + eye).astype(BF)

        cols = slice(p * wide, (p + 1) * wide)
        out_ref[:, cols] = jnp.dot(
            left_ref[...], held[:, cols], preferred_element_type=F32
        ).astype(BF)


def in_vmem(x):
    return pltpu.with_memory_space_constraint(x, pltpu.VMEM)


def in_hbm(x):
    return pltpu.with_memory_space_constraint(x, pltpu.HBM)


VMEM_SPEC = pl.BlockSpec(memory_space=pltpu.VMEM)
SMEM_SPEC = pl.BlockSpec(memory_space=pltpu.SMEM)
HBM_SPEC = pl.BlockSpec(memory_space=pltpu.HBM)


def load_dot(left, right, pattern, place, with_diag):
    rows = left.shape[0]
    depth, cols = right.shape
    return pl.pallas_call(
        lambda *refs: load_kernel(with_diag, *refs),
        in_specs=[SMEM_SPEC, SMEM_SPEC, VMEM_SPEC, HBM_SPEC],
        out_specs=[VMEM_SPEC, VMEM_SPEC],
        out_shape=[pltpu.VMEM((rows, cols), BF), pltpu.VMEM((depth, cols), BF)],
        scratch_shapes=[pltpu.SemaphoreType.DMA((3,))],
        compiler_params=pltpu.CompilerParams(vmem_limit_bytes=SMALL),
        cost_estimate=pl.CostEstimate(
            flops=2 * rows * cols * depth, bytes_accessed=2 * cols * depth, transcendentals=0
        ),
        name="load_dot",
    )(pattern, place, in_vmem(left), in_hbm(right))


def dot_kernel(left_ref, right_ref, out_ref):
    wide = 4 * BLK
    for p in range(right_ref.shape[1] // wide):
        cols = slice(p * wide, (p + 1) * wide)
        out_ref[:, cols] = jnp.dot(
            left_ref[...], right_ref[:, cols], preferred_element_type=F32
        ).astype(out_ref.dtype)


def dot(left, right, dtype):
    rows, depth = left.shape
    cols = right.shape[1]
    return pl.pallas_call(
        dot_kernel,
        in_specs=[VMEM_SPEC, VMEM_SPEC],
        out_specs=VMEM_SPEC,
        out_shape=pltpu.VMEM((rows, cols), dtype),
        compiler_params=pltpu.CompilerParams(vmem_limit_bytes=SMALL),
        cost_estimate=pl.CostEstimate(
            flops=2 * rows * cols * depth, bytes_accessed=2 * rows * (cols + depth), transcendentals=0
        ),
        name="dot",
    )(in_vmem(left), right)


def sum_kernel(parts_ref, out_ref):
    n, _, cols = parts_ref.shape
    for j in range(cols // BLK):
        lanes = slice(j * BLK, (j + 1) * BLK)
        total = parts_ref[0, :, lanes].astype(F32)
        for k in range(1, n):
            total = total + parts_ref[k, :, lanes].astype(F32)
        for k in range(n):
            out_ref[k, :, lanes] = total.astype(BF)


def summed(parts):
    return pl.pallas_call(
        sum_kernel,
        in_specs=[VMEM_SPEC],
        out_specs=VMEM_SPEC,
        out_shape=pltpu.VMEM(parts.shape, BF),
        compiler_params=pltpu.CompilerParams(vmem_limit_bytes=SMALL),
        name="sum",
    )(in_vmem(parts))


def finish_kernel(keep_ref, where_ref, parts_ref, two_ref, out_ref):
    n, rows, cols = parts_ref.shape
    for at in range(0, rows, 8):
        block_row = (where_ref[2] + at) // BLK
        for j in range(cols // BLK):
            lanes = slice(j * BLK, (j + 1) * BLK)
            four = parts_ref[0, at : at + 8, lanes].astype(F32)
            for k in range(1, n):
                four = four + parts_ref[k, at : at + 8, lanes].astype(F32)
            value = 3.0 * two_ref[0, at : at + 8, lanes].astype(F32) - 2.0 * four
            kept = keep_ref[block_row, where_ref[3] + j] > 0
            out_ref[at : at + 8, lanes] = jnp.where(kept, value, jnp.zeros_like(value)).astype(BF)


def finish(parts, two, keep, place):
    return pl.pallas_call(
        finish_kernel,
        in_specs=[SMEM_SPEC, SMEM_SPEC, VMEM_SPEC, VMEM_SPEC],
        out_specs=VMEM_SPEC,
        out_shape=jax.ShapeDtypeStruct(two.shape[1:], BF),
        compiler_params=pltpu.CompilerParams(vmem_limit_bytes=SMALL),
        name="finish",
    )(keep, place, in_vmem(parts), in_vmem(two))


def exchange(parts, axis):
    return lax.all_to_all(parts, axis, 0, 0, tiled=False)


def swap(x):
    return lax.ppermute(x, "core", [(0, 1), (1, 0)])


def body(density, margin, density_mask, margin_mask, keep_mask):
    side = density.shape[0]
    nr = NX * NY
    r = lax.axis_index(ROW)
    z = lax.axis_index("z")
    core = lax.axis_index("core")
    c = z * NC + core
    blocks = side // BLK
    slab = SLAB_BLK * BLK
    piece = slab // (NZ * NC)
    place = jnp.stack([r * blocks, c * blocks, c * piece, r * blocks]).astype(jnp.int32)

    half = NZ * piece

    top = slab_halves(density, density_mask, slab, piece)
    mine = jnp.where(core == 0, top[0], lax.ppermute(top[1], ("z", "core"), [(0, 1)]))
    got = jnp.where(z == 0, mine[0], jnp.zeros_like(mine[0]))
    for d in ORDER:
        dealt = lax.ppermute(mine[d], "z", [(0, d)])
        got = got + dealt
    own = exchange(jnp.broadcast_to(got[None], (NZ, piece, side)), "z").reshape(half, side)

    def over_rows(first, second):
        part = jnp.concatenate([first, second]).reshape(nr, slab // nr, side)
        return exchange(summed(exchange(part, ROW)), ROW).reshape(slab, side)

    def over_cols(kept, sent):
        part = (kept + sent.astype(F32)).astype(BF)
        return exchange(part.reshape(NZ, piece, side), "z")

    other = swap(own)
    first, over = load_dot(own, margin, margin_mask, place, True)
    left = over_rows(first, dot(other, over, BF))
    sent, dense = load_dot(left[half:], density, density_mask, place, False)
    sent = swap(sent)
    twos = summed(over_cols(dot(left[:half], dense, F32), sent))
    own = exchange(twos, "z").reshape(half, side)
    other = swap(own)
    first = dot(own, over, BF)
    left = over_rows(first, dot(other, over, BF))
    sent = swap(dot(left[half:], dense, BF))
    parts = over_cols(dot(left[:half], dense, F32), sent)
    return finish(parts, twos, keep_mask, place)


def solution(mesh):
    grid = Mesh(mesh.devices.reshape(NX, NY, NZ, NC), ("x", "y", "z", "core"))
    dn, mg = P(("z", "core"), ROW), P(ROW, ("z", "core"))
    return jax.shard_map(
        body, mesh=grid, in_specs=(dn, mg, dn, mg, P()), out_specs=dn, check_vma=False
    )
```

profile of v0, /device:TPU:2, one launch (start us, length us, event | category | flops | bytes accessed | tf_op | source)
XLA Modules:
  0.0 220.0 jit_solution(16423373217494089474)
XLA Ops:
  0.0 0.7 copy-done
  0.7 2.0 slab.1
  2.7 1.8 collective-permute-start
  4.5 1.6 collective-permute-done
  6.1 0.1 broadcast_select_fusion
  6.2 1.3 collective-permute-start.1
  7.5 4.5 %collective-permute-start.7 = (bf16[24,1536]{1,0:T(8,128)(2,1)S(1)}, bf16[24,1536]{1,0:T(8,128)(2,1)S(1)}, u32[]{:S(2)}, u32[]{:S(2)}) collective-permute-start(bf16[24,1536]{1,0:T(8,128)(2,1)S(1)} %get-tuple-element.22), channel_id=1, source_target_pairs={{0,8},{1,9},{16,24},{17,25},{32,40},{33,41},{48,56},{49,57},{64,72... | collective-permute-start | bytes 221192 | tf_op jit(solution)/shard_map/ppermute | solution.py:226
  12.0 1.3 collective-permute-start.6
  13.3 1.3 collective-permute-start.5
  14.6 1.3 collective-permute-start.4
  15.9 1.3 collective-permute-start.3
  17.3 1.3 collective-permute-start.2
  18.6 0.0 copy-start.2
  18.6 1.1 collective-permute-done.3
  19.7 1.0 collective-permute-done.2
  20.8 23.0 %all_to_all.40 = bf16[8,24,1536]{2,1,0:T(8,128)(2,1)S(1)} all-to-all(bf16[8,24,1536]{2,1,0:T(8,128)(2,1)S(1)} %broadcast_in_dim.10), channel_id=1, replica_groups=mesh['x'=4,'y'=4,'z'=8,'core'=2] {'z'}, dimensions={0} | all-to-all | bytes 1179648 | tf_op jit(solution)/shard_map/all_to_all | solution.py:201
  43.8 0.1 pad_add_fusion.refs_1_.where_ref
  43.9 4.8 %load_dot.2 = (bf16[192,1536]{1,0:T(8,128)(2,1)S(1)}, bf16[1536,1536]{1,0:T(8,128)(2,1)S(1)}) custom-call(s32[12,12]{1,0:T(8,128)S(1)} %copy-done.2, s32[4]{0:T(128)S(1)} %pad_add_fusion.refs_1_.where_ref, bf16[192,1536]{1,0:T(8,128)(2,1)S(1)} %bitcast.49, bf16[1536,1536]{1,0:T(8,128)(2,1)} %refs_3_.2), custom_call_target="tpu_custom_call" | custom-call | flops 905969664 | bytes 4718592 | tf_op jit(solution)/shard_map/load_dot/pallas_call | solution.py:114
  48.7 1.1 dot.6
  49.8 0.1 pad_maximum_fusion
  49.9 24.9 %all_to_all.41.parts_ref = bf16[16,24,1536]{2,1,0:T(8,128)(2,1)S(1)} all-to-all(bf16[16,24,1536]{2,1,0:T(8,128)(2,1)S(1)} %bitcast.51), channel_id=1, replica_groups=mesh['x'=4,'y'=4,'z'=8,'core'=2] {'x','y'}, dimensions={0} | all-to-all | bytes 2359296 | tf_op jit(solution)/shard_map/all_to_all | solution.py:201
  74.8 0.2 sum.3
  74.9 21.3 %all_to_all.42 = bf16[16,24,1536]{2,1,0:T(8,128)(2,1)S(1)} all-to-all(bf16[16,24,1536]{2,1,0:T(8,128)(2,1)S(1)} %sum.3), channel_id=1, replica_groups=mesh['x'=4,'y'=4,'z'=8,'core'=2] {'x','y'}, dimensions={0} | all-to-all | bytes 2359296 | tf_op jit(solution)/shard_map/all_to_all | solution.py:201
  96.3 0.1 fusion.9
  96.4 0.6 copy-done.1
  97.0 4.7 %load_dot.3 = (bf16[192,1536]{1,0:T(8,128)(2,1)S(1)}, bf16[1536,1536]{1,0:T(8,128)(2,1)S(1)}) custom-call(s32[12,12]{1,0:T(8,128)S(1)} %copy-done.1, s32[4]{0:T(128)S(1)} %pad_add_fusion.refs_1_.where_ref, bf16[192,1536]{1,0:T(8,128)(2,1)S(1)} %bitcast.50, bf16[1536,1536]{1,0:T(8,128)(2,1)} %refs_3_.3), custom_call_target="tpu_custom_call" | custom-call | flops 905969664 | bytes 4718592 | tf_op jit(solution)/shard_map/load_dot/pallas_call | solution.py:114
  101.6 0.1 collective-permute-start.9
  101.7 1.1 dot.7
  102.8 0.9 collective-permute-done.9
  103.7 0.1 add_convert_fusion.1
  103.8 21.9 %all_to_all.43.parts_ref = bf16[8,24,1536]{2,1,0:T(8,128)(2,1)S(1)} all-to-all(bf16[8,24,1536]{2,1,0:T(8,128)(2,1)S(1)} %bitcast.53), channel_id=1, replica_groups=mesh['x'=4,'y'=4,'z'=8,'core'=2] {'z'}, dimensions={0} | all-to-all | bytes 1179648 | tf_op jit(solution)/shard_map/all_to_all | solution.py:201
  125.7 0.1 sum.4.two_ref
  125.8 21.2 %all_to_all.44 = bf16[8,24,1536]{2,1,0:T(8,128)(2,1)S(1)} all-to-all(bf16[8,24,1536]{2,1,0:T(8,128)(2,1)S(1)} %sum.4.two_ref), channel_id=1, replica_groups=mesh['x'=4,'y'=4,'z'=8,'core'=2] {'z'}, dimensions={0} | all-to-all | bytes 1179648 | tf_op jit(solution)/shard_map/all_to_all | solution.py:201
  147.0 1.1 dot.8
  148.1 0.9 collective-permute-done.10.left_ref
  149.0 1.1 dot.9
  150.1 0.1 pad_maximum_fusion.1
  150.1 22.1 %all_to_all.45.parts_ref = bf16[16,24,1536]{2,1,0:T(8,128)(2,1)S(1)} all-to-all(bf16[16,24,1536]{2,1,0:T(8,128)(2,1)S(1)} %bitcast.52), channel_id=1, replica_groups=mesh['x'=4,'y'=4,'z'=8,'core'=2] {'x','y'}, dimensions={0} | all-to-all | bytes 2359296 | tf_op jit(solution)/shard_map/all_to_all | solution.py:201
  172.3 0.2 sum.5
  172.5 20.9 %all_to_all.46 = bf16[16,24,1536]{2,1,0:T(8,128)(2,1)S(1)} all-to-all(bf16[16,24,1536]{2,1,0:T(8,128)(2,1)S(1)} %sum.5), channel_id=1, replica_groups=mesh['x'=4,'y'=4,'z'=8,'core'=2] {'x','y'}, dimensions={0} | all-to-all | bytes 2359296 | tf_op jit(solution)/shard_map/all_to_all | solution.py:201
  193.4 0.1 fusion.8
  193.5 1.1 dot.11
  194.6 0.1 collective-permute-start.11
  194.7 1.1 dot.10
  195.8 0.9 collective-permute-done.11
  196.7 0.1 add_convert_fusion
  196.8 21.9 %all_to_all.47.parts_ref = bf16[8,24,1536]{2,1,0:T(8,128)(2,1)S(1)} all-to-all(bf16[8,24,1536]{2,1,0:T(8,128)(2,1)S(1)} %bitcast.54), channel_id=1, replica_groups=mesh['x'=4,'y'=4,'z'=8,'core'=2] {'z'}, dimensions={0} | all-to-all | bytes 1179648 | tf_op jit(solution)/shard_map/all_to_all | solution.py:201
  218.7 1.4 finish.1
  (16 shorter events, 0.2 us)
Async XLA Ops:
  0.0 0.7 copy-start
  2.7 3.4 %collective-permute-start = (bf16[8,24,1536]{2,1,0:T(8,128)(2,1)S(1)}, bf16[8,24,1536]{2,1,0:T(8,128)(2,1)S(1)}, u32[]{:S(2)}, u32[]{:S(2)}) collective-permute-start(bf16[8,24,1536]{2,1,0:T(8,128)(2,1)S(1)} %get-tuple-element.12), channel_id=1, source_target_pairs={{0,1},{16,17},{32,33},{48,49},{64,65},{80,81},{96,97},{112,113},{1... | collective-permute-start | bytes 1769480 | tf_op jit(solution)/shard_map/ppermute | solution.py:223
  6.2 9.7 %collective-permute-start.1 = (bf16[24,1536]{1,0:T(8,128)(2,1)S(1)}, bf16[24,1536]{1,0:T(8,128)(2,1)S(1)}, u32[]{:S(2)}, u32[]{:S(2)}) collective-permute-start(bf16[24,1536]{1,0:T(8,128)(2,1)S(1)} %get-tuple-element.21), channel_id=1, source_target_pairs={{0,2},{1,3},{16,18},{17,19},{32,34},{33,35},{48,50},{49,51},{64,66... | collective-permute-start | bytes 221192 | tf_op jit(solution)/shard_map/ppermute | solution.py:226
  7.5 9.7 %collective-permute-start.7 = (bf16[24,1536]{1,0:T(8,128)(2,1)S(1)}, bf16[24,1536]{1,0:T(8,128)(2,1)S(1)}, u32[]{:S(2)}, u32[]{:S(2)}) collective-permute-start(bf16[24,1536]{1,0:T(8,128)(2,1)S(1)} %get-tuple-element.22), channel_id=1, source_target_pairs={{0,8},{1,9},{16,24},{17,25},{32,40},{33,41},{48,56},{49,57},{64,72... | collective-permute-start | bytes 221192 | tf_op jit(solution)/shard_map/ppermute | solution.py:226
  12.0 6.6 %collective-permute-start.6 = (bf16[24,1536]{1,0:T(8,128)(2,1)S(1)}, bf16[24,1536]{1,0:T(8,128)(2,1)S(1)}, u32[]{:S(2)}, u32[]{:S(2)}) collective-permute-start(bf16[24,1536]{1,0:T(8,128)(2,1)S(1)} %get-tuple-element.23), channel_id=1, source_target_pairs={{0,14},{1,15},{16,30},{17,31},{32,46},{33,47},{48,62},{49,63},{64,... | collective-permute-start | bytes 221192 | tf_op jit(solution)/shard_map/ppermute | solution.py:226
  13.3 5.3 %collective-permute-start.5 = (bf16[24,1536]{1,0:T(8,128)(2,1)S(1)}, bf16[24,1536]{1,0:T(8,128)(2,1)S(1)}, u32[]{:S(2)}, u32[]{:S(2)}) collective-permute-start(bf16[24,1536]{1,0:T(8,128)(2,1)S(1)} %get-tuple-element.24), channel_id=1, source_target_pairs={{0,10},{1,11},{16,26},{17,27},{32,42},{33,43},{48,58},{49,59},{64,... | collective-permute-start | bytes 221192 | tf_op jit(solution)/shard_map/ppermute | solution.py:226
  14.6 4.0 %collective-permute-start.4 = (bf16[24,1536]{1,0:T(8,128)(2,1)S(1)}, bf16[24,1536]{1,0:T(8,128)(2,1)S(1)}, u32[]{:S(2)}, u32[]{:S(2)}) collective-permute-start(bf16[24,1536]{1,0:T(8,128)(2,1)S(1)} %get-tuple-element.25), channel_id=1, source_target_pairs={{0,12},{1,13},{16,28},{17,29},{32,44},{33,45},{48,60},{49,61},{64,... | collective-permute-start | bytes 221192 | tf_op jit(solution)/shard_map/ppermute | solution.py:226
  15.9 3.8 %collective-permute-start.3 = (bf16[24,1536]{1,0:T(8,128)(2,1)S(1)}, bf16[24,1536]{1,0:T(8,128)(2,1)S(1)}, u32[]{:S(2)}, u32[]{:S(2)}) collective-permute-start(bf16[24,1536]{1,0:T(8,128)(2,1)S(1)} %get-tuple-element.26), channel_id=1, source_target_pairs={{0,6},{1,7},{16,22},{17,23},{32,38},{33,39},{48,54},{49,55},{64,70... | collective-permute-start | bytes 221192 | tf_op jit(solution)/shard_map/ppermute | solution.py:226
  17.3 3.4 %collective-permute-start.2 = (bf16[24,1536]{1,0:T(8,128)(2,1)S(1)}, bf16[24,1536]{1,0:T(8,128)(2,1)S(1)}, u32[]{:S(2)}, u32[]{:S(2)}) collective-permute-start(bf16[24,1536]{1,0:T(8,128)(2,1)S(1)} %get-tuple-element.27), channel_id=1, source_target_pairs={{0,4},{1,5},{16,20},{17,21},{32,36},{33,37},{48,52},{49,53},{64,68... | collective-permute-start | bytes 221192 | tf_op jit(solution)/shard_map/ppermute | solution.py:226
  18.6 25.3 %copy-start.2 = (s32[12,12]{1,0:T(8,128)S(1)}, s32[12,12]{1,0:T(8,128)}, u32[]{:S(2)}) copy-start(s32[12,12]{1,0:T(8,128)} %refs_0_.4) | copy-start | bytes 1732
  43.8 4.9 %collective-permute-start.8 = (bf16[192,1536]{1,0:T(8,128)(2,1)S(1)}, bf16[192,1536]{1,0:T(8,128)(2,1)S(1)}, u32[]{:S(2)}, u32[]{:S(2)}) collective-permute-start(bf16[192,1536]{1,0:T(8,128)(2,1)S(1)} %bitcast.48), channel_id=1, source_target_pairs={{0,1},{1,0},{2,3},{3,2},{4,5},{5,4},{6,7},{7,6},{8,9},{9,8},{10,11... | collective-permute-start | bytes 1769480 | tf_op jit(solution)/shard_map/ppermute | solution.py:205
  96.3 0.7 copy-start.1
  101.6 2.1 collective-permute-start.9
  147.0 2.0 collective-permute-start.10
  194.6 2.1 collective-permute-start.11
  196.8 21.9 %copy-start.3 = (s32[3,192]{1,0:T(4,128)S(1)}, s32[3,192]{1,0:T(4,128)}, u32[]{:S(2)}) copy-start(s32[3,192]{1,0:T(4,128)} %keep_ref.1) | copy-start | bytes 6916
where the time goes:
time: 222 us; the launch traced here: 220 us
  blocking collectives  177 us (80%)
  Pallas kernels  19.8 us (9%)
  starting transfers between devices  14.2 us (6%)
  waiting for transfers between devices  6.36 us (3%)
    all_to_all x8, blocking collectives, exchange(): return lax.all_to_all(parts, axis, 0, 0, tiled=False)  177 us
    ppermute x7, starting transfers between devices, body(): dealt = lax.ppermute(mine[d], 'z', [(0, d)])  12.3 us
    pallas_call x2, Pallas kernels, load_dot(): pl.pallas_call(lambda *refs: load_kernel(with_diag, *refs), in_specs=[SME...  9.44 us
    pallas_call x6, Pallas kernels, dot(): pl.pallas_call(dot_kernel, in_specs=[VMEM_SPEC, VMEM_SPEC], out_specs=VME...  6.52 us
  transfers between devices with their start and end apart: 12, of which 6 were waited for; matrix products, arithmetic and copies ran while one was open for 0% of the time, Pallas kernels for 4%

commit v1 on v0

--- a/solution.py
+++ b/solution.py
@@ -52,47 +52,60 @@
         scratch_shapes=[pltpu.VMEM((slab, cols), BF), pltpu.SemaphoreType.DMA((SLAB_BLK,))],
         compiler_params=pltpu.CompilerParams(vmem_limit_bytes=SMALL),
         name="slab",
-    )(pattern, pltpu.with_memory_space_constraint(tile, pltpu.HBM))
-
-
-def load_kernel(with_diag, pattern_ref, where_ref, left_ref, right_ref, out_ref, held, sems):
+    )(pltpu.with_memory_space_constraint(pattern, pltpu.HBM), pltpu.with_memory_space_constraint(tile, pltpu.HBM))
+
+
+def grid_place():
+    row = lax.axis_index("x") * NY + lax.axis_index("y")
+    return row, lax.axis_index("z") * NC + lax.axis_index("core")
+
+
+def load_kernel(with_diag, pattern_ref, left_ref, right_ref, out_ref, held, sems):
     depth, width = held.shape
+    row, col = grid_place()
+    diagonal = row == col
     parts = sems.shape[0]
     wide = width // parts
-    copies = [
-        pltpu.make_async_copy(
-            right_ref.at[:, pl.ds(j * wide, wide)], held.at[:, pl.ds(j * wide, wide)], sems.at[j]
-        )
-        for j in range(parts)
-    ]
-    copies[0].start()
-    copies[1].start()
+    tall = depth // sems.shape[1]
+    copies = []
     for p in range(parts):
-        copies[p].wait()
-        if p + 2 < parts:
-            copies[p + 2].start()
-        for j in range(p * wide // BLK, (p + 1) * wide // BLK):
-            for i in range(depth // BLK):
-                here = (slice(i * BLK, (i + 1) * BLK), slice(j * BLK, (j + 1) * BLK))
-
-                @pl.when(pattern_ref[i, j] <= 0)
-                def _():
-                    held[here] = jnp.zeros((BLK, BLK), BF)
-
+        for q in range(sems.shape[1]):
+            span = (pl.ds(q * tall, tall), pl.ds(p * wide, wide))
+            copies.append(
+                pltpu.make_async_copy(right_ref.at[span], held.at[span], sems.at[p, q])
+            )
+            copies[-1].start()
+    for p in range(parts):
+        for q in range(sems.shape[1]):
+            copies[p * sems.shape[1] + q].wait()
+        blocks = range(p * wide // BLK, (p + 1) * wide // BLK)
+        if with_diag:
+
+            @pl.when(diagonal)
+            def _():
+                eye = (
+                    lax.broadcasted_iota(jnp.int32, (BLK, BLK), 0)
+                    == lax.broadcasted_iota(jnp.int32, (BLK, BLK), 1)
+                ).astype(F32)
+                for j in blocks:
+                    here = (slice(j * BLK, (j + 1) * BLK), slice(j * BLK, (j + 1) * BLK))
+                    block = jnp.where(pattern_ref[j, j] > 0, held[here].astype(F32), 0.0)
+                    held[here] = (block + eye).astype(BF)
+
+        strips = []
+        for i in range(depth // BLK):
+            strip = []
+            for j in blocks:
+                block = held[i * BLK : (i + 1) * BLK, j * BLK : (j + 1) * BLK]
+                stored = pattern_ref[i, j] > 0
                 if with_diag and i == j:
-
-                    @pl.when(where_ref[0] == where_ref[1])
-                    def _():
-                        eye = (
-                            lax.broadcasted_iota(jnp.int32, (BLK, BLK), 0)
-                            == lax.broadcasted_iota(jnp.int32, (BLK, BLK), 1)
-                        ).astype(F32)
-                        held[here] = (held[here].astype(F32) + eye).astype(BF)
-
+                    stored = jnp.logical_or(stored, diagonal)
+                strip.append(jnp.where(stored, block, jnp.zeros_like(block)))
+            strips.append(jnp.concatenate(strip, axis=1))
+        values = jnp.concatenate(strips, axis=0)
         cols = slice(p * wide, (p + 1) * wide)
-        out_ref[:, cols] = jnp.dot(
-            left_ref[...], held[:, cols], preferred_element_type=F32
-        ).astype(BF)
+        held[:, cols] = values
+        out_ref[:, cols] = jnp.dot(left_ref[...], values, preferred_element_type=F32).astype(BF)
 
 
 def in_vmem(x):
@@ -108,21 +121,21 @@
 HBM_SPEC = pl.BlockSpec(memory_space=pltpu.HBM)
 
 
-def load_dot(left, right, pattern, place, with_diag):
+def load_dot(left, right, pattern, with_diag):
     rows = left.shape[0]
     depth, cols = right.shape
     return pl.pallas_call(
         lambda *refs: load_kernel(with_diag, *refs),
-        in_specs=[SMEM_SPEC, SMEM_SPEC, VMEM_SPEC, HBM_SPEC],
+        in_specs=[SMEM_SPEC, VMEM_SPEC, HBM_SPEC],
         out_specs=[VMEM_SPEC, VMEM_SPEC],
         out_shape=[pltpu.VMEM((rows, cols), BF), pltpu.VMEM((depth, cols), BF)],
-        scratch_shapes=[pltpu.SemaphoreType.DMA((3,))],
+        scratch_shapes=[pltpu.SemaphoreType.DMA((3, 4))],
         compiler_params=pltpu.CompilerParams(vmem_limit_bytes=SMALL),
         cost_estimate=pl.CostEstimate(
             flops=2 * rows * cols * depth, bytes_accessed=2 * cols * depth, transcendentals=0
         ),
         name="load_dot",
-    )(pattern, place, in_vmem(left), in_hbm(right))
+    )(in_hbm(pattern), in_vmem(left), in_hbm(right))
 
 
 def dot_kernel(left_ref, right_ref, out_ref):
@@ -172,29 +185,30 @@
     )(in_vmem(parts))
 
 
-def finish_kernel(keep_ref, where_ref, parts_ref, two_ref, out_ref):
+def finish_kernel(keep_ref, parts_ref, two_ref, out_ref):
     n, rows, cols = parts_ref.shape
+    row, col = grid_place()
     for at in range(0, rows, 8):
-        block_row = (where_ref[2] + at) // BLK
+        block_row = (col * rows + at) // BLK
         for j in range(cols // BLK):
             lanes = slice(j * BLK, (j + 1) * BLK)
             four = parts_ref[0, at : at + 8, lanes].astype(F32)
             for k in range(1, n):
                 four = four + parts_ref[k, at : at + 8, lanes].astype(F32)
             value = 3.0 * two_ref[0, at : at + 8, lanes].astype(F32) - 2.0 * four
-            kept = keep_ref[block_row, where_ref[3] + j] > 0
+            kept = keep_ref[block_row, row * (cols // BLK) + j] > 0
             out_ref[at : at + 8, lanes] = jnp.where(kept, value, jnp.zeros_like(value)).astype(BF)
 
 
-def finish(parts, two, keep, place):
+def finish(parts, two, keep):
     return pl.pallas_call(
         finish_kernel,
-        in_specs=[SMEM_SPEC, SMEM_SPEC, VMEM_SPEC, VMEM_SPEC],
+        in_specs=[SMEM_SPEC, VMEM_SPEC, VMEM_SPEC],
         out_specs=VMEM_SPEC,
         out_shape=jax.ShapeDtypeStruct(two.shape[1:], BF),
         compiler_params=pltpu.CompilerParams(vmem_limit_bytes=SMALL),
         name="finish",
-    )(keep, place, in_vmem(parts), in_vmem(two))
+    )(in_hbm(keep), in_vmem(parts), in_vmem(two))
 
 
 def exchange(parts, axis):
@@ -208,15 +222,10 @@
 def body(density, margin, density_mask, margin_mask, keep_mask):
     side = density.shape[0]
     nr = NX * NY
-    r = lax.axis_index(ROW)
     z = lax.axis_index("z")
     core = lax.axis_index("core")
-    c = z * NC + core
-    blocks = side // BLK
     slab = SLAB_BLK * BLK
     piece = slab // (NZ * NC)
-    place = jnp.stack([r * blocks, c * blocks, c * piece, r * blocks]).astype(jnp.int32)
-
     half = NZ * piece
 
     top = slab_halves(density, density_mask, slab, piece)
@@ -236,9 +245,9 @@
         return exchange(part.reshape(NZ, piece, side), "z")
 
     other = swap(own)
-    first, over = load_dot(own, margin, margin_mask, place, True)
+    first, over = load_dot(own, margin, margin_mask, True)
     left = over_rows(first, dot(other, over, BF))
-    sent, dense = load_dot(left[half:], density, density_mask, place, False)
+    sent, dense = load_dot(left[half:], density, density_mask, False)
     sent = swap(sent)
     twos = summed(over_cols(dot(left[:half], dense, F32), sent))
     own = exchange(twos, "z").reshape(half, side)
@@ -247,7 +256,7 @@
     left = over_rows(first, dot(other, over, BF))
     sent = swap(dot(left[half:], dense, BF))
     parts = over_cols(dot(left[:half], dense, F32), sent)
-    return finish(parts, twos, keep_mask, place)
+    return finish(parts, twos, keep_mask)
 
 
 def solution(mesh):

time: 222 us -> 219 us (0.986)
  transfers between devices with their start and end apart: 12 -> 12, of which waited for: 6 -> 6; matrix products, arithmetic and copies ran while one was open for 0% -> 0% of each run, Pallas kernels for 4% -> 3%
where the time goes in v1:
time: 219 us; the launch traced here: 217 us
  blocking collectives  177 us (81%)
  Pallas kernels  18.2 us (8%)
  starting transfers between devices  14.2 us (6%)
  waiting for transfers between devices  6.37 us (3%)
    all_to_all x8, blocking collectives, exchange(): return lax.all_to_all(parts, axis, 0, 0, tiled=False)  177 us
    ppermute x7, starting transfers between devices, body(): dealt = lax.ppermute(mine[d], 'z', [(0, d)])  12.3 us
    pallas_call x2, Pallas kernels, load_dot(): pl.pallas_call(lambda *refs: load_kernel(with_diag, *refs), in_specs=[SME...  7.63 us
    pallas_call x6, Pallas kernels, dot(): pl.pallas_call(dot_kernel, in_specs=[VMEM_SPEC, VMEM_SPEC], out_specs=VME...  6.52 us
  transfers between devices with their start and end apart: 12, of which 6 were waited for; matrix products, arithmetic and copies ran while one was open for 0% of the time, Pallas kernels for 3%

profile of v1, /device:TPU:2, one launch (start us, length us, event | category | flops | bytes accessed | tf_op | source)
XLA Modules:
  0.0 216.9 jit_solution(17834937782154449774)
XLA Ops:
  0.0 2.1 slab.1
  2.2 1.8 collective-permute-start
  3.9 1.6 collective-permute-done
  5.5 0.1 broadcast_select_fusion
  5.6 1.3 collective-permute-start.1
  6.9 4.5 %collective-permute-start.7 = (bf16[24,1536]{1,0:T(8,128)(2,1)S(1)}, bf16[24,1536]{1,0:T(8,128)(2,1)S(1)}, u32[]{:S(2)}, u32[]{:S(2)}) collective-permute-start(bf16[24,1536]{1,0:T(8,128)(2,1)S(1)} %get-tuple-element.22), channel_id=1, source_target_pairs={{0,8},{1,9},{16,24},{17,25},{32,40},{33,41},{48,56},{49,57},{64,72... | collective-permute-start | bytes 221192 | tf_op jit(solution)/shard_map/ppermute | solution.py:235
  11.5 1.3 collective-permute-start.6
  12.8 1.3 collective-permute-start.5
  14.1 1.3 collective-permute-start.4
  15.4 1.3 collective-permute-start.3
  16.7 1.3 collective-permute-start.2
  18.0 0.0 collective-permute-done.4
  18.0 1.1 collective-permute-done.3
  19.1 1.0 collective-permute-done.2
  20.2 23.0 %all_to_all.40 = bf16[8,24,1536]{2,1,0:T(8,128)(2,1)S(1)} all-to-all(bf16[8,24,1536]{2,1,0:T(8,128)(2,1)S(1)} %broadcast_in_dim.10), channel_id=1, replica_groups=mesh['x'=4,'y'=4,'z'=8,'core'=2] {'z'}, dimensions={0} | all-to-all | bytes 1179648 | tf_op jit(solution)/shard_map/all_to_all | solution.py:215
  43.2 0.0 collective-permute-start.8
  43.2 3.8 %load_dot.2 = (bf16[192,1536]{1,0:T(8,128)(2,1)S(1)}, bf16[1536,1536]{1,0:T(8,128)(2,1)S(1)}) custom-call(s32[12,12]{1,0:T(8,128)} %refs_0_.4, bf16[192,1536]{1,0:T(8,128)(2,1)S(1)} %bitcast.46, bf16[1536,1536]{1,0:T(8,128)(2,1)} %refs_2_.2), custom_call_target="tpu_custom_call" | custom-call | flops 905969664 | bytes 4718592 | tf_op jit(solution)/shard_map/load_dot/pallas_call | solution.py:127
  47.0 0.0 collective-permute-done.8.left_ref
  47.0 1.1 dot.6
  48.1 0.1 pad_maximum_fusion
  48.2 24.9 %all_to_all.41.parts_ref = bf16[16,24,1536]{2,1,0:T(8,128)(2,1)S(1)} all-to-all(bf16[16,24,1536]{2,1,0:T(8,128)(2,1)S(1)} %bitcast.48), channel_id=1, replica_groups=mesh['x'=4,'y'=4,'z'=8,'core'=2] {'x','y'}, dimensions={0} | all-to-all | bytes 2359296 | tf_op jit(solution)/shard_map/all_to_all | solution.py:215
  73.1 0.2 sum.3
  73.3 21.3 %all_to_all.42 = bf16[16,24,1536]{2,1,0:T(8,128)(2,1)S(1)} all-to-all(bf16[16,24,1536]{2,1,0:T(8,128)(2,1)S(1)} %sum.3), channel_id=1, replica_groups=mesh['x'=4,'y'=4,'z'=8,'core'=2] {'x','y'}, dimensions={0} | all-to-all | bytes 2359296 | tf_op jit(solution)/shard_map/all_to_all | solution.py:215
  94.6 0.1 fusion.9
  94.7 3.8 %load_dot.3 = (bf16[192,1536]{1,0:T(8,128)(2,1)S(1)}, bf16[1536,1536]{1,0:T(8,128)(2,1)S(1)}) custom-call(s32[12,12]{1,0:T(8,128)} %refs_0_.5, bf16[192,1536]{1,0:T(8,128)(2,1)S(1)} %bitcast.47, bf16[1536,1536]{1,0:T(8,128)(2,1)} %refs_2_.3), custom_call_target="tpu_custom_call" | custom-call | flops 905969664 | bytes 4718592 | tf_op jit(solution)/shard_map/load_dot/pallas_call | solution.py:127
  98.5 0.1 collective-permute-start.9
  98.6 1.1 dot.7
  99.7 0.9 collective-permute-done.9
  100.6 0.1 add_convert_fusion.1
  100.7 21.9 %all_to_all.43.parts_ref = bf16[8,24,1536]{2,1,0:T(8,128)(2,1)S(1)} all-to-all(bf16[8,24,1536]{2,1,0:T(8,128)(2,1)S(1)} %bitcast.50), channel_id=1, replica_groups=mesh['x'=4,'y'=4,'z'=8,'core'=2] {'z'}, dimensions={0} | all-to-all | bytes 1179648 | tf_op jit(solution)/shard_map/all_to_all | solution.py:215
  122.5 0.1 sum.4.two_ref
  122.6 21.2 %all_to_all.44 = bf16[8,24,1536]{2,1,0:T(8,128)(2,1)S(1)} all-to-all(bf16[8,24,1536]{2,1,0:T(8,128)(2,1)S(1)} %sum.4.two_ref), channel_id=1, replica_groups=mesh['x'=4,'y'=4,'z'=8,'core'=2] {'z'}, dimensions={0} | all-to-all | bytes 1179648 | tf_op jit(solution)/shard_map/all_to_all | solution.py:215
  143.8 0.0 collective-permute-start.10
  143.8 1.1 dot.8
  144.9 0.9 collective-permute-done.10.left_ref
  145.8 1.1 dot.9
  146.9 0.1 pad_maximum_fusion.1
  147.0 22.1 %all_to_all.45.parts_ref = bf16[16,24,1536]{2,1,0:T(8,128)(2,1)S(1)} all-to-all(bf16[16,24,1536]{2,1,0:T(8,128)(2,1)S(1)} %bitcast.49), channel_id=1, replica_groups=mesh['x'=4,'y'=4,'z'=8,'core'=2] {'x','y'}, dimensions={0} | all-to-all | bytes 2359296 | tf_op jit(solution)/shard_map/all_to_all | solution.py:215
  169.1 0.2 sum.5
  169.2 20.9 %all_to_all.46 = bf16[16,24,1536]{2,1,0:T(8,128)(2,1)S(1)} all-to-all(bf16[16,24,1536]{2,1,0:T(8,128)(2,1)S(1)} %sum.5), channel_id=1, replica_groups=mesh['x'=4,'y'=4,'z'=8,'core'=2] {'x','y'}, dimensions={0} | all-to-all | bytes 2359296 | tf_op jit(solution)/shard_map/all_to_all | solution.py:215
  190.2 0.1 fusion.8
  190.2 1.1 dot.11
  191.3 0.1 collective-permute-start.11
  191.4 1.1 dot.10
  192.5 0.9 collective-permute-done.11
  193.4 0.1 add_convert_fusion
  193.6 21.9 %all_to_all.47.parts_ref = bf16[8,24,1536]{2,1,0:T(8,128)(2,1)S(1)} all-to-all(bf16[8,24,1536]{2,1,0:T(8,128)(2,1)S(1)} %bitcast.51), channel_id=1, replica_groups=mesh['x'=4,'y'=4,'z'=8,'core'=2] {'z'}, dimensions={0} | all-to-all | bytes 1179648 | tf_op jit(solution)/shard_map/all_to_all | solution.py:215
  215.4 1.5 finish.1
  (7 shorter events, 0.1 us)
Async XLA Ops:
  2.2 3.4 %collective-permute-start = (bf16[8,24,1536]{2,1,0:T(8,128)(2,1)S(1)}, bf16[8,24,1536]{2,1,0:T(8,128)(2,1)S(1)}, u32[]{:S(2)}, u32[]{:S(2)}) collective-permute-start(bf16[8,24,1536]{2,1,0:T(8,128)(2,1)S(1)} %get-tuple-element.12), channel_id=1, source_target_pairs={{0,1},{16,17},{32,33},{48,49},{64,65},{80,81},{96,97},{112,113},{1... | collective-permute-start | bytes 1769480 | tf_op jit(solution)/shard_map/ppermute | solution.py:232
  5.6 9.7 %collective-permute-start.1 = (bf16[24,1536]{1,0:T(8,128)(2,1)S(1)}, bf16[24,1536]{1,0:T(8,128)(2,1)S(1)}, u32[]{:S(2)}, u32[]{:S(2)}) collective-permute-start(bf16[24,1536]{1,0:T(8,128)(2,1)S(1)} %get-tuple-element.21), channel_id=1, source_target_pairs={{0,2},{1,3},{16,18},{17,19},{32,34},{33,35},{48,50},{49,51},{64,66... | collective-permute-start | bytes 221192 | tf_op jit(solution)/shard_map/ppermute | solution.py:235
  6.9 9.7 %collective-permute-start.7 = (bf16[24,1536]{1,0:T(8,128)(2,1)S(1)}, bf16[24,1536]{1,0:T(8,128)(2,1)S(1)}, u32[]{:S(2)}, u32[]{:S(2)}) collective-permute-start(bf16[24,1536]{1,0:T(8,128)(2,1)S(1)} %get-tuple-element.22), channel_id=1, source_target_pairs={{0,8},{1,9},{16,24},{17,25},{32,40},{33,41},{48,56},{49,57},{64,72... | collective-permute-start | bytes 221192 | tf_op jit(solution)/shard_map/ppermute | solution.py:235
  11.5 6.5 %collective-permute-start.6 = (bf16[24,1536]{1,0:T(8,128)(2,1)S(1)}, bf16[24,1536]{1,0:T(8,128)(2,1)S(1)}, u32[]{:S(2)}, u32[]{:S(2)}) collective-permute-start(bf16[24,1536]{1,0:T(8,128)(2,1)S(1)} %get-tuple-element.23), channel_id=1, source_target_pairs={{0,14},{1,15},{16,30},{17,31},{32,46},{33,47},{48,62},{49,63},{64,... | collective-permute-start | bytes 221192 | tf_op jit(solution)/shard_map/ppermute | solution.py:235
  12.8 5.2 %collective-permute-start.5 = (bf16[24,1536]{1,0:T(8,128)(2,1)S(1)}, bf16[24,1536]{1,0:T(8,128)(2,1)S(1)}, u32[]{:S(2)}, u32[]{:S(2)}) collective-permute-start(bf16[24,1536]{1,0:T(8,128)(2,1)S(1)} %get-tuple-element.24), channel_id=1, source_target_pairs={{0,10},{1,11},{16,26},{17,27},{32,42},{33,43},{48,58},{49,59},{64,... | collective-permute-start | bytes 221192 | tf_op jit(solution)/shard_map/ppermute | solution.py:235
  14.1 4.0 %collective-permute-start.4 = (bf16[24,1536]{1,0:T(8,128)(2,1)S(1)}, bf16[24,1536]{1,0:T(8,128)(2,1)S(1)}, u32[]{:S(2)}, u32[]{:S(2)}) collective-permute-start(bf16[24,1536]{1,0:T(8,128)(2,1)S(1)} %get-tuple-element.25), channel_id=1, source_target_pairs={{0,12},{1,13},{16,28},{17,29},{32,44},{33,45},{48,60},{49,61},{64,... | collective-permute-start | bytes 221192 | tf_op jit(solution)/shard_map/ppermute | solution.py:235
  15.4 3.8 %collective-permute-start.3 = (bf16[24,1536]{1,0:T(8,128)(2,1)S(1)}, bf16[24,1536]{1,0:T(8,128)(2,1)S(1)}, u32[]{:S(2)}, u32[]{:S(2)}) collective-permute-start(bf16[24,1536]{1,0:T(8,128)(2,1)S(1)} %get-tuple-element.26), channel_id=1, source_target_pairs={{0,6},{1,7},{16,22},{17,23},{32,38},{33,39},{48,54},{49,55},{64,70... | collective-permute-start | bytes 221192 | tf_op jit(solution)/shard_map/ppermute | solution.py:235
  16.7 3.4 %collective-permute-start.2 = (bf16[24,1536]{1,0:T(8,128)(2,1)S(1)}, bf16[24,1536]{1,0:T(8,128)(2,1)S(1)}, u32[]{:S(2)}, u32[]{:S(2)}) collective-permute-start(bf16[24,1536]{1,0:T(8,128)(2,1)S(1)} %get-tuple-element.27), channel_id=1, source_target_pairs={{0,4},{1,5},{16,20},{17,21},{32,36},{33,37},{48,52},{49,53},{64,68... | collective-permute-start | bytes 221192 | tf_op jit(solution)/shard_map/ppermute | solution.py:235
  43.2 3.8 %collective-permute-start.8 = (bf16[192,1536]{1,0:T(8,128)(2,1)S(1)}, bf16[192,1536]{1,0:T(8,128)(2,1)S(1)}, u32[]{:S(2)}, u32[]{:S(2)}) collective-permute-start(bf16[192,1536]{1,0:T(8,128)(2,1)S(1)} %bitcast.45), channel_id=1, source_target_pairs={{0,1},{1,0},{2,3},{3,2},{4,5},{5,4},{6,7},{7,6},{8,9},{9,8},{10,11... | collective-permute-start | bytes 1769480 | tf_op jit(solution)/shard_map/ppermute | solution.py:219
  98.5 2.1 collective-permute-start.9
  143.8 2.0 collective-permute-start.10
  191.3 2.1 collective-permute-start.11

commit v2 on v1

--- a/solution.py
+++ b/solution.py
@@ -60,52 +60,37 @@
     return row, lax.axis_index("z") * NC + lax.axis_index("core")
 
 
-def load_kernel(with_diag, pattern_ref, left_ref, right_ref, out_ref, held, sems):
-    depth, width = held.shape
+def load_kernel(over_mask, dense_mask, over_ref, dense_ref, over_out, dense_out, sems):
     row, col = grid_place()
     diagonal = row == col
-    parts = sems.shape[0]
-    wide = width // parts
-    tall = depth // sems.shape[1]
+    depth, width = over_out.shape
+    strips = sems.shape[1]
+    tall = depth // strips
+    sets = ((over_mask, over_ref, over_out), (dense_mask, dense_ref, dense_out))
     copies = []
-    for p in range(parts):
-        for q in range(sems.shape[1]):
-            span = (pl.ds(q * tall, tall), pl.ds(p * wide, wide))
-            copies.append(
-                pltpu.make_async_copy(right_ref.at[span], held.at[span], sems.at[p, q])
-            )
+    for which, (_, source, held) in enumerate(sets):
+        for q in range(strips):
+            span = pl.ds(q * tall, tall)
+            copies.append(pltpu.make_async_copy(source.at[span], held.at[span], sems.at[which, q]))
             copies[-1].start()
-    for p in range(parts):
-        for q in range(sems.shape[1]):
-            copies[p * sems.shape[1] + q].wait()
-        blocks = range(p * wide // BLK, (p + 1) * wide // BLK)
-        if with_diag:
-
-            @pl.when(diagonal)
-            def _():
-                eye = (
-                    lax.broadcasted_iota(jnp.int32, (BLK, BLK), 0)
-                    == lax.broadcasted_iota(jnp.int32, (BLK, BLK), 1)
-                ).astype(F32)
-                for j in blocks:
-                    here = (slice(j * BLK, (j + 1) * BLK), slice(j * BLK, (j + 1) * BLK))
-                    block = jnp.where(pattern_ref[j, j] > 0, held[here].astype(F32), 0.0)
-                    held[here] = (block + eye).astype(BF)
-
-        strips = []
+    eye = (
+        lax.broadcasted_iota(jnp.int32, (BLK, BLK), 0)
+        == lax.broadcasted_iota(jnp.int32, (BLK, BLK), 1)
+    ).astype(F32)
+    for which, (mask, _, held) in enumerate(sets):
+        for q in range(strips):
+            copies[which * strips + q].wait()
+            for i in range(q * tall // BLK, (q + 1) * tall // BLK):
+                for j in range(width // BLK):
+                    here = (slice(i * BLK, (i + 1) * BLK), slice(j * BLK, (j + 1) * BLK))
+                    block = held[here]
+                    held[here] = jnp.where(mask[i, j] > 0, block, jnp.zeros_like(block))
+
+    @pl.when(diagonal)
+    def _():
         for i in range(depth // BLK):
-            strip = []
-            for j in blocks:
-                block = held[i * BLK : (i + 1) * BLK, j * BLK : (j + 1) * BLK]
-                stored = pattern_ref[i, j] > 0
-                if with_diag and i == j:
-                    stored = jnp.logical_or(stored, diagonal)
-                strip.append(jnp.where(stored, block, jnp.zeros_like(block)))
-            strips.append(jnp.concatenate(strip, axis=1))
-        values = jnp.concatenate(strips, axis=0)
-        cols = slice(p * wide, (p + 1) * wide)
-        held[:, cols] = values
-        out_ref[:, cols] = jnp.dot(left_ref[...], values, preferred_element_type=F32).astype(BF)
+            here = (slice(i * BLK, (i + 1) * BLK), slice(i * BLK, (i + 1) * BLK))
+            over_out[here] = (over_out[here].astype(F32) + eye).astype(BF)
 
 
 def in_vmem(x):
@@ -121,21 +106,19 @@
 HBM_SPEC = pl.BlockSpec(memory_space=pltpu.HBM)
 
 
-def load_dot(left, right, pattern, with_diag):
-    rows = left.shape[0]
-    depth, cols = right.shape
-    return pl.pallas_call(
-        lambda *refs: load_kernel(with_diag, *refs),
-        in_specs=[SMEM_SPEC, VMEM_SPEC, HBM_SPEC],
+def load(margin, density, margin_mask, density_mask):
+    return pl.pallas_call(
+        load_kernel,
+        in_specs=[SMEM_SPEC, SMEM_SPEC, HBM_SPEC, HBM_SPEC],
         out_specs=[VMEM_SPEC, VMEM_SPEC],
-        out_shape=[pltpu.VMEM((rows, cols), BF), pltpu.VMEM((depth, cols), BF)],
-        scratch_shapes=[pltpu.SemaphoreType.DMA((3, 4))],
+        out_shape=[pltpu.VMEM(margin.shape, BF), pltpu.VMEM(density.shape, BF)],
+        scratch_shapes=[pltpu.SemaphoreType.DMA((2, 4))],
         compiler_params=pltpu.CompilerParams(vmem_limit_bytes=SMALL),
         cost_estimate=pl.CostEstimate(
-            flops=2 * rows * cols * depth, bytes_accessed=2 * cols * depth, transcendentals=0
+            flops=2 * margin.size, bytes_accessed=4 * margin.size, transcendentals=0
         ),
-        name="load_dot",
-    )(in_hbm(pattern), in_vmem(left), in_hbm(right))
+        name="load",
+    )(in_hbm(margin_mask), in_hbm(density_mask), in_hbm(margin), in_hbm(density))
 
 
 def dot_kernel(left_ref, right_ref, out_ref):
@@ -234,6 +217,7 @@
     for d in ORDER:
         dealt = lax.ppermute(mine[d], "z", [(0, d)])
         got = got + dealt
+    over, dense = load(margin, density, margin_mask, density_mask)
     own = exchange(jnp.broadcast_to(got[None], (NZ, piece, side)), "z").reshape(half, side)
 
     def over_rows(first, second):
@@ -245,10 +229,9 @@
         return exchange(part.reshape(NZ, piece, side), "z")
 
     other = swap(own)
-    first, over = load_dot(own, margin, margin_mask, True)
+    first = dot(own, over, BF)
     left = over_rows(first, dot(other, over, BF))
-    sent, dense = load_dot(left[half:], density, density_mask, False)
-    sent = swap(sent)
+    sent = swap(dot(left[half:], dense, BF))
     twos = summed(over_cols(dot(left[:half], dense, F32), sent))
     own = exchange(twos, "z").reshape(half, side)
     other = swap(own)

time: 219 us -> 219 us (level)
    pallas_call x2 -> x1, Pallas kernels: 7.63 us -> 4.98 us  [load(): pl.pallas_call(load_kernel, in_specs=[SMEM_SPEC, SMEM_SPEC, HBM_SPEC, HBM...]
    pallas_call x6 -> x8, Pallas kernels: 6.52 us -> 8.69 us  [dot(): pl.pallas_call(dot_kernel, in_specs=[VMEM_SPEC, VMEM_SPEC], out_specs=VME...]
  transfers between devices with their start and end apart: 12 -> 12, of which waited for: 6 -> 6; matrix products, arithmetic and copies ran while one was open for 0% -> 0% of each run, Pallas kernels for 3% -> 4%
where the time goes in v2:
time: 219 us; the launch traced here: 216 us
  blocking collectives  177 us (81%)
  Pallas kernels  17.8 us (8%)
  starting transfers between devices  14.2 us (6%)
  waiting for transfers between devices  6.37 us (3%)
    all_to_all x8, blocking collectives, exchange(): return lax.all_to_all(parts, axis, 0, 0, tiled=False)  177 us
    ppermute x7, starting transfers between devices, body(): dealt = lax.ppermute(mine[d], 'z', [(0, d)])  12.3 us
    pallas_call x8, Pallas kernels, dot(): pl.pallas_call(dot_kernel, in_specs=[VMEM_SPEC, VMEM_SPEC], out_specs=VME...  8.69 us
    pallas_call x1, Pallas kernels, load(): pl.pallas_call(load_kernel, in_specs=[SMEM_SPEC, SMEM_SPEC, HBM_SPEC, HBM...  4.98 us
  transfers between devices with their start and end apart: 12, of which 6 were waited for; matrix products, arithmetic and copies ran while one was open for 0% of the time, Pallas kernels for 4%

profile of v2, /device:TPU:2, one launch (start us, length us, event | category | flops | bytes accessed | tf_op | source)
XLA Modules:
  0.0 216.5 jit_solution(8777088559232274631)
XLA Ops:
  0.0 2.1 slab.1
  2.2 1.8 collective-permute-start
  3.9 1.6 collective-permute-done
  5.5 0.1 broadcast_select_fusion
  5.6 1.3 collective-permute-start.1
  6.9 4.5 %collective-permute-start.7 = (bf16[24,1536]{1,0:T(8,128)(2,1)S(1)}, bf16[24,1536]{1,0:T(8,128)(2,1)S(1)}, u32[]{:S(2)}, u32[]{:S(2)}) collective-permute-start(bf16[24,1536]{1,0:T(8,128)(2,1)S(1)} %get-tuple-element.18), channel_id=1, source_target_pairs={{0,8},{1,9},{16,24},{17,25},{32,40},{33,41},{48,56},{49,57},{64,72... | collective-permute-start | bytes 221192 | tf_op jit(solution)/shard_map/ppermute | solution.py:218
  11.5 1.3 collective-permute-start.6
  12.8 1.3 collective-permute-start.5
  14.1 1.3 collective-permute-start.4
  15.4 1.3 collective-permute-start.3
  16.7 1.3 collective-permute-start.2
  18.0 0.0 collective-permute-done.4
  18.0 1.1 collective-permute-done.3
  19.1 1.0 collective-permute-done.2
  20.2 23.0 %all_to_all.40 = bf16[8,24,1536]{2,1,0:T(8,128)(2,1)S(1)} all-to-all(bf16[8,24,1536]{2,1,0:T(8,128)(2,1)S(1)} %broadcast_in_dim.10), channel_id=1, replica_groups=mesh['x'=4,'y'=4,'z'=8,'core'=2] {'z'}, dimensions={0} | all-to-all | bytes 1179648 | tf_op jit(solution)/shard_map/all_to_all | solution.py:198
  43.2 0.0 collective-permute-start.8
  43.2 5.0 %load.1 = (bf16[1536,1536]{1,0:T(8,128)(2,1)S(1)}, bf16[1536,1536]{1,0:T(8,128)(2,1)S(1)}) custom-call(s32[12,12]{1,0:T(8,128)} %over_mask.1, s32[12,12]{1,0:T(8,128)} %dense_mask.1, bf16[1536,1536]{1,0:T(8,128)(2,1)} %over_ref.1, bf16[1536,1536]{1,0:T(8,128)(2,1)} %dense_ref.1), custom_call_target="tpu_custom_call" | custom-call | flops 4718592 | bytes 9437184 | tf_op jit(solution)/shard_map/load/pallas_call | solution.py:110
  48.2 1.1 dot.8
  49.3 0.0 collective-permute-done.8.left_ref
  49.3 1.1 dot.9
  50.4 0.1 pad_maximum_fusion
  50.5 24.9 %all_to_all.41.parts_ref = bf16[16,24,1536]{2,1,0:T(8,128)(2,1)S(1)} all-to-all(bf16[16,24,1536]{2,1,0:T(8,128)(2,1)S(1)} %bitcast.48), channel_id=1, replica_groups=mesh['x'=4,'y'=4,'z'=8,'core'=2] {'x','y'}, dimensions={0} | all-to-all | bytes 2359296 | tf_op jit(solution)/shard_map/all_to_all | solution.py:198
  75.4 0.2 sum.3
  75.5 21.3 %all_to_all.42 = bf16[16,24,1536]{2,1,0:T(8,128)(2,1)S(1)} all-to-all(bf16[16,24,1536]{2,1,0:T(8,128)(2,1)S(1)} %sum.3), channel_id=1, replica_groups=mesh['x'=4,'y'=4,'z'=8,'core'=2] {'x','y'}, dimensions={0} | all-to-all | bytes 2359296 | tf_op jit(solution)/shard_map/all_to_all | solution.py:198
  96.9 0.1 fusion.9
  97.0 1.1 dot.11
  98.1 0.1 collective-permute-start.9
  98.2 1.1 dot.10
  99.2 0.9 collective-permute-done.9
  100.1 0.1 add_convert_fusion.1
  100.3 21.9 %all_to_all.43.parts_ref = bf16[8,24,1536]{2,1,0:T(8,128)(2,1)S(1)} all-to-all(bf16[8,24,1536]{2,1,0:T(8,128)(2,1)S(1)} %bitcast.50), channel_id=1, replica_groups=mesh['x'=4,'y'=4,'z'=8,'core'=2] {'z'}, dimensions={0} | all-to-all | bytes 1179648 | tf_op jit(solution)/shard_map/all_to_all | solution.py:198
  122.1 0.1 sum.4.two_ref
  122.2 21.2 %all_to_all.44 = bf16[8,24,1536]{2,1,0:T(8,128)(2,1)S(1)} all-to-all(bf16[8,24,1536]{2,1,0:T(8,128)(2,1)S(1)} %sum.4.two_ref), channel_id=1, replica_groups=mesh['x'=4,'y'=4,'z'=8,'core'=2] {'z'}, dimensions={0} | all-to-all | bytes 1179648 | tf_op jit(solution)/shard_map/all_to_all | solution.py:198
  143.4 1.1 dot.12
  144.5 0.9 collective-permute-done.10.left_ref
  145.4 1.1 dot.13
  146.5 0.1 pad_maximum_fusion.1
  146.6 22.1 %all_to_all.45.parts_ref = bf16[16,24,1536]{2,1,0:T(8,128)(2,1)S(1)} all-to-all(bf16[16,24,1536]{2,1,0:T(8,128)(2,1)S(1)} %bitcast.49), channel_id=1, replica_groups=mesh['x'=4,'y'=4,'z'=8,'core'=2] {'x','y'}, dimensions={0} | all-to-all | bytes 2359296 | tf_op jit(solution)/shard_map/all_to_all | solution.py:198
  168.6 0.2 sum.5
  168.8 20.9 %all_to_all.46 = bf16[16,24,1536]{2,1,0:T(8,128)(2,1)S(1)} all-to-all(bf16[16,24,1536]{2,1,0:T(8,128)(2,1)S(1)} %sum.5), channel_id=1, replica_groups=mesh['x'=4,'y'=4,'z'=8,'core'=2] {'x','y'}, dimensions={0} | all-to-all | bytes 2359296 | tf_op jit(solution)/shard_map/all_to_all | solution.py:198
  189.8 0.1 fusion.8
  189.8 1.1 dot.15
  190.9 0.1 collective-permute-start.11
  191.0 1.1 dot.14
  192.1 0.9 collective-permute-done.11
  193.0 0.1 add_convert_fusion
  193.1 21.9 %all_to_all.47.parts_ref = bf16[8,24,1536]{2,1,0:T(8,128)(2,1)S(1)} all-to-all(bf16[8,24,1536]{2,1,0:T(8,128)(2,1)S(1)} %bitcast.51), channel_id=1, replica_groups=mesh['x'=4,'y'=4,'z'=8,'core'=2] {'z'}, dimensions={0} | all-to-all | bytes 1179648 | tf_op jit(solution)/shard_map/all_to_all | solution.py:198
  215.0 1.5 finish.1
  (8 shorter events, 0.1 us)
Async XLA Ops:
  2.2 3.4 %collective-permute-start = (bf16[8,24,1536]{2,1,0:T(8,128)(2,1)S(1)}, bf16[8,24,1536]{2,1,0:T(8,128)(2,1)S(1)}, u32[]{:S(2)}, u32[]{:S(2)}) collective-permute-start(bf16[8,24,1536]{2,1,0:T(8,128)(2,1)S(1)} %get-tuple-element.10), channel_id=1, source_target_pairs={{0,1},{16,17},{32,33},{48,49},{64,65},{80,81},{96,97},{112,113},{1... | collective-permute-start | bytes 1769480 | tf_op jit(solution)/shard_map/ppermute | solution.py:215
  5.6 9.7 %collective-permute-start.1 = (bf16[24,1536]{1,0:T(8,128)(2,1)S(1)}, bf16[24,1536]{1,0:T(8,128)(2,1)S(1)}, u32[]{:S(2)}, u32[]{:S(2)}) collective-permute-start(bf16[24,1536]{1,0:T(8,128)(2,1)S(1)} %get-tuple-element.17), channel_id=1, source_target_pairs={{0,2},{1,3},{16,18},{17,19},{32,34},{33,35},{48,50},{49,51},{64,66... | collective-permute-start | bytes 221192 | tf_op jit(solution)/shard_map/ppermute | solution.py:218
  6.9 9.7 %collective-permute-start.7 = (bf16[24,1536]{1,0:T(8,128)(2,1)S(1)}, bf16[24,1536]{1,0:T(8,128)(2,1)S(1)}, u32[]{:S(2)}, u32[]{:S(2)}) collective-permute-start(bf16[24,1536]{1,0:T(8,128)(2,1)S(1)} %get-tuple-element.18), channel_id=1, source_target_pairs={{0,8},{1,9},{16,24},{17,25},{32,40},{33,41},{48,56},{49,57},{64,72... | collective-permute-start | bytes 221192 | tf_op jit(solution)/shard_map/ppermute | solution.py:218
  11.5 6.5 %collective-permute-start.6 = (bf16[24,1536]{1,0:T(8,128)(2,1)S(1)}, bf16[24,1536]{1,0:T(8,128)(2,1)S(1)}, u32[]{:S(2)}, u32[]{:S(2)}) collective-permute-start(bf16[24,1536]{1,0:T(8,128)(2,1)S(1)} %get-tuple-element.19), channel_id=1, source_target_pairs={{0,14},{1,15},{16,30},{17,31},{32,46},{33,47},{48,62},{49,63},{64,... | collective-permute-start | bytes 221192 | tf_op jit(solution)/shard_map/ppermute | solution.py:218
  12.8 5.2 %collective-permute-start.5 = (bf16[24,1536]{1,0:T(8,128)(2,1)S(1)}, bf16[24,1536]{1,0:T(8,128)(2,1)S(1)}, u32[]{:S(2)}, u32[]{:S(2)}) collective-permute-start(bf16[24,1536]{1,0:T(8,128)(2,1)S(1)} %get-tuple-element.20), channel_id=1, source_target_pairs={{0,10},{1,11},{16,26},{17,27},{32,42},{33,43},{48,58},{49,59},{64,... | collective-permute-start | bytes 221192 | tf_op jit(solution)/shard_map/ppermute | solution.py:218
  14.1 4.0 %collective-permute-start.4 = (bf16[24,1536]{1,0:T(8,128)(2,1)S(1)}, bf16[24,1536]{1,0:T(8,128)(2,1)S(1)}, u32[]{:S(2)}, u32[]{:S(2)}) collective-permute-start(bf16[24,1536]{1,0:T(8,128)(2,1)S(1)} %get-tuple-element.21), channel_id=1, source_target_pairs={{0,12},{1,13},{16,28},{17,29},{32,44},{33,45},{48,60},{49,61},{64,... | collective-permute-start | bytes 221192 | tf_op jit(solution)/shard_map/ppermute | solution.py:218
  15.4 3.8 %collective-permute-start.3 = (bf16[24,1536]{1,0:T(8,128)(2,1)S(1)}, bf16[24,1536]{1,0:T(8,128)(2,1)S(1)}, u32[]{:S(2)}, u32[]{:S(2)}) collective-permute-start(bf16[24,1536]{1,0:T(8,128)(2,1)S(1)} %get-tuple-element.22), channel_id=1, source_target_pairs={{0,6},{1,7},{16,22},{17,23},{32,38},{33,39},{48,54},{49,55},{64,70... | collective-permute-start | bytes 221192 | tf_op jit(solution)/shard_map/ppermute | solution.py:218
  16.7 3.4 %collective-permute-start.2 = (bf16[24,1536]{1,0:T(8,128)(2,1)S(1)}, bf16[24,1536]{1,0:T(8,128)(2,1)S(1)}, u32[]{:S(2)}, u32[]{:S(2)}) collective-permute-start(bf16[24,1536]{1,0:T(8,128)(2,1)S(1)} %get-tuple-element.23), channel_id=1, source_target_pairs={{0,4},{1,5},{16,20},{17,21},{32,36},{33,37},{48,52},{49,53},{64,68... | collective-permute-start | bytes 221192 | tf_op jit(solution)/shard_map/ppermute | solution.py:218
  43.2 6.1 %collective-permute-start.8 = (bf16[192,1536]{1,0:T(8,128)(2,1)S(1)}, bf16[192,1536]{1,0:T(8,128)(2,1)S(1)}, u32[]{:S(2)}, u32[]{:S(2)}) collective-permute-start(bf16[192,1536]{1,0:T(8,128)(2,1)S(1)} %bitcast.40), channel_id=1, source_target_pairs={{0,1},{1,0},{2,3},{3,2},{4,5},{5,4},{6,7},{7,6},{8,9},{9,8},{10,11... | collective-permute-start | bytes 1769480 | tf_op jit(solution)/shard_map/ppermute | solution.py:202
  98.1 2.1 collective-permute-start.9
  143.4 2.0 collective-permute-start.10
  190.9 2.1 collective-permute-start.11
